TPU v7x, 256 devices: a whole 4x4x8 slice. The times are simulated.
256 devices in a mesh: seq: 16 (over x, z_lo), ch: 16 (over z_hi, y, core).
Axes of the slice: x: 4, y: 4, z: 8 (z_hi: 2, z_lo: 4; z = z_hi * 4 + z_lo), core: 2. Of those that a mesh axis runs over, the one named last changes fastest.
Arguments:
- signal: bfloat16 [8192, 2048], P('seq', 'ch'), may hold values from -6 to 6
- filter_raw: bfloat16 [8192, 2048], P('seq', 'ch'), may hold values from -6 to 6
- gate: bfloat16 [8192, 2048], P('seq', 'ch'), may hold values from -6 to 6
- d_out: bfloat16 [8192, 2048], P('seq', 'ch'), may hold values from -6 to 6
- w_first: bfloat16 [32, 64, 64], P('ch'), may hold values from -0.75 to 0.75
- w_second: bfloat16 [64, 32, 32], P('ch'), may hold values from -1 to 1
Outputs:
- grad_signal: bfloat16 [8192, 2048], P('seq', 'ch')
- grad_filter: bfloat16 [8192, 2048], P('seq', 'ch')
- grad_gate: bfloat16 [8192, 2048], P('seq', 'ch')
- grad_first: float32 [32, 64, 64], P('ch', 'seq')
- grad_second: float32 [64, 32, 32], P('ch', 'seq')
All inputs are finite; a program needn't handle non-finite values.
Results may differ from a plain program's by a relative error of at most 0.02.
Values may be sent and summed in bfloat16 or wider, within the bound.
No kernel may reach another device: no remote copies, remote signals or barrier semaphores. Data moves between devices by JAX's collectives and lax.ppermute only.
A program may use at most 64 MiB of HBM per device.

v0:
```python
import math
import jax
import jax.numpy as jnp
from jax import lax
from jax.sharding import PartitionSpec as P

HIGHEST = lax.Precision.HIGHEST


def counting(count):
    return jnp.arange(count, dtype=jnp.int32)


def phase_table(row_ids, col_ids, length, sign):
    angles = (
        2.0 * math.pi / length * (row_ids[:, None] * col_ids[None, :] % length).astype(jnp.float32)
    )
    return (jnp.cos(angles), sign * jnp.sin(angles))


def contract(form, table, real_part, imag_part):
    cosine, sine = table
    out_real = jnp.einsum(form, cosine, real_part, precision=HIGHEST) - jnp.einsum(
        form, sine, imag_part, precision=HIGHEST
    )
    out_imag = jnp.einsum(form, cosine, imag_part, precision=HIGHEST) + jnp.einsum(
        form, sine, real_part, precision=HIGHEST
    )
    return (out_real, out_imag)


def rotate(cosine, sine, real_part, imag_part):
    return (real_part * cosine - imag_part * sine, real_part * sine + imag_part * cosine)


def factors(length):
    return (length // 128, 128)


def local_forward(real_part, imag_part):
    fields, group, rows, width = real_part.shape
    outer, inner = factors(rows)
    real_part = real_part.reshape(fields, group, outer, inner, width)
    imag_part = imag_part.reshape(fields, group, outer, inner, width)
    real_part, imag_part = contract(
        "qa,fkabc->fkqbc",
        phase_table(counting(outer), counting(outer), outer, -1.0),
        real_part,
        imag_part,
    )
    cosine, sine = phase_table(counting(outer), counting(inner), rows, -1.0)
    real_part, imag_part = rotate(cosine[:, :, None], sine[:, :, None], real_part, imag_part)
    return contract(
        "rb,fkqbc->fkqrc",
        phase_table(counting(inner), counting(inner), inner, -1.0),
        real_part,
        imag_part,
    )


def local_inverse(real_part, imag_part):
    fields, group, outer, inner, width = real_part.shape
    rows = outer * inner
    real_part, imag_part = contract(
        "br,fkqrc->fkqbc",
        phase_table(counting(inner), counting(inner), inner, 1.0),
        real_part,
        imag_part,
    )
    cosine, sine = phase_table(counting(outer), counting(inner), rows, 1.0)
    real_part, imag_part = rotate(cosine[:, :, None], sine[:, :, None], real_part, imag_part)
    real_part, imag_part = contract(
        "aq,fkqbc->fkabc",
        phase_table(counting(outer), counting(outer), outer, 1.0),
        real_part,
        imag_part,
    )
    return (
        real_part.reshape(fields, group, rows, width),
        imag_part.reshape(fields, group, rows, width),
    )


def forward_transform(fields):
    devices = lax.axis_size("seq")
    count, rows, width = fields.shape
    piece = rows // devices
    span = 2 * devices
    whole = span * rows
    parts = lax.all_to_all(fields[:, None], "seq", split_axis=2, concat_axis=1, tiled=True)
    cosine, sine = phase_table(counting(span), counting(devices), span, -1.0)
    real_part = jnp.einsum("ka,fabc->fkbc", cosine, parts, precision=HIGHEST)
    imag_part = jnp.einsum("ka,fabc->fkbc", sine, parts, precision=HIGHEST)
    positions = lax.axis_index("seq") * piece + counting(piece)
    cosine, sine = phase_table(counting(span), positions, whole, -1.0)
    real_part, imag_part = rotate(cosine[:, :, None], sine[:, :, None], real_part, imag_part)
    spectrum = lax.all_to_all(
        jnp.stack([real_part, imag_part], axis=1), "seq", split_axis=2, concat_axis=3, tiled=True
    )
    return local_forward(spectrum[:, 0], spectrum[:, 1])


def inverse_transform(real_part, imag_part):
    devices = lax.axis_size("seq")
    real_part, imag_part = local_inverse(real_part, imag_part)
    group = real_part.shape[1]
    rows = real_part.shape[2]
    span = 2 * devices
    whole = span * rows
    classes = lax.axis_index("seq") * group + counting(group)
    cosine, sine = phase_table(classes, counting(rows), whole, 1.0)
    real_part, imag_part = rotate(cosine[:, :, None], sine[:, :, None], real_part, imag_part)
    gathered = lax.all_to_all(
        jnp.stack([real_part, imag_part], axis=1), "seq", split_axis=3, concat_axis=2, tiled=True
    )
    cosine, sine = phase_table(counting(devices), counting(span), span, 1.0)
    inverse_scale = 1.0 / whole
    out_real = (
        jnp.einsum("ak,fkbc->fabc", cosine, gathered[:, 0], precision=HIGHEST)
        - jnp.einsum("ak,fkbc->fabc", sine, gathered[:, 1], precision=HIGHEST)
    ) * inverse_scale
    slab = lax.all_to_all(out_real, "seq", split_axis=1, concat_axis=2, tiled=True)
    return slab[:, 0]


def adjoint_spectra(spectra_real, spectra_imag, incoming_real, incoming_imag):
    toward_signal_real = spectra_real[1] * incoming_real + spectra_imag[1] * incoming_imag
    toward_signal_imag = spectra_real[1] * incoming_imag - spectra_imag[1] * incoming_real
    toward_filter_real = spectra_real[0] * incoming_real + spectra_imag[0] * incoming_imag
    toward_filter_imag = spectra_real[0] * incoming_imag - spectra_imag[0] * incoming_real
    return (toward_signal_real, toward_signal_imag, toward_filter_real, toward_filter_imag)


def shards(signal, filter_raw, gate, d_out, w_first, w_second):
    rows, width = signal.shape
    scale = float(rows * lax.axis_size("seq")) ** (-0.5)
    signal_wide = signal.astype(jnp.float32)
    kernel = filter_raw.astype(jnp.float32) * scale
    spectra_real, spectra_imag = forward_transform(jnp.stack([signal_wide, kernel]))
    mixed_real = spectra_real[0] * spectra_real[1] - spectra_imag[0] * spectra_imag[1]
    mixed_imag = spectra_real[0] * spectra_imag[1] + spectra_imag[0] * spectra_real[1]
    conv = inverse_transform(mixed_real[None], mixed_imag[None])[0].astype(jnp.bfloat16)
    gate_wide = gate.astype(jnp.float32)
    product = (conv.astype(jnp.float32) * gate_wide).astype(jnp.bfloat16)
    blocks = w_first.shape[0]
    block = w_first.shape[1]
    product_blocks = product.reshape(rows, blocks, block)
    first_mix = jnp.einsum(
        "tij,ijk->tik", product_blocks, w_first, preferred_element_type=jnp.float32
    ).astype(jnp.bfloat16)
    received = lax.all_to_all(first_mix, "ch", split_axis=2, concat_axis=1, tiled=True)
    incoming = d_out.reshape(rows, w_second.shape[0], w_second.shape[1])
    second_back = jnp.einsum(
        "tko,kio->tki", incoming, w_second, preferred_element_type=jnp.float32
    ).astype(jnp.bfloat16)
    grad_second = jnp.einsum("tik,tko->kio", received, incoming, preferred_element_type=jnp.float32)
    returned = lax.all_to_all(second_back, "ch", split_axis=2, concat_axis=1, tiled=True)
    grad_product = jnp.einsum(
        "tki,ijk->tij", returned, w_first, preferred_element_type=jnp.float32
    ).reshape(rows, width)
    grad_first = jnp.einsum(
        "tij,tki->ijk", product_blocks, returned, preferred_element_type=jnp.float32
    )
    grad_gate = (grad_product * conv.astype(jnp.float32)).astype(jnp.bfloat16)
    grad_conv = grad_product * gate_wide
    incoming_real, incoming_imag = forward_transform(grad_conv[None])
    sig_real, sig_imag, fil_real, fil_imag = adjoint_spectra(
        spectra_real, spectra_imag, incoming_real[0], incoming_imag[0]
    )
    results = inverse_transform(jnp.stack([sig_real, fil_real]), jnp.stack([sig_imag, fil_imag]))
    grad_signal = results[0].astype(jnp.bfloat16)
    grad_filter = (results[1] * scale).astype(jnp.bfloat16)
    grad_first = lax.psum_scatter(
        grad_first.astype(jnp.bfloat16), "seq", scatter_dimension=1, tiled=True
    ).astype(jnp.float32)
    grad_second = lax.psum_scatter(grad_second, "seq", scatter_dimension=1, tiled=True)
    return (grad_signal, grad_filter, grad_gate, grad_first, grad_second)


def solution(mesh):
    in_specs = (
        P("seq", "ch"),
        P("seq", "ch"),
        P("seq", "ch"),
        P("seq", "ch"),
        P("ch", None, None),
        P("ch", None, None),
    )
    out_specs = (
        P("seq", "ch"),
        P("seq", "ch"),
        P("seq", "ch"),
        P("ch", "seq", None),
        P("ch", "seq", None),
    )
    return jax.shard_map(shards, mesh=mesh, in_specs=in_specs, out_specs=out_specs, check_vma=False)
```

profile of v0, /device:TPU:8, one launch (start us, length us, event | category | flops | bytes accessed | tf_op | source)
XLA Modules:
  0.0 462.7 jit_solution(11425884564633815950)
XLA Ops:
  2.8 20.1 %all_to_all.147 = bf16[512,4,32]{0,1,2:T(4,128)(2,1)S(1)} all-to-all(bf16[512,4,32]{0,1,2:T(4,128)(2,1)S(1)} %copy.234), channel_id=1, replica_groups=mesh['seq'=16,'ch'=16] {'ch'}, dimensions={2} | all-to-all | bytes 262144 | tf_op jit(solution)/shard_map/all_to_all | solution.py:157
  24.1 5.8 %all-to-all-start.3 = ((f32[1,1,512,128]{3,1,0,2:T(1,128)}), f32[1,1,512,128]{3,1,0,2:T(1,128)S(1)}, u32[]{:S(2)}, u32[]{:S(2)}) async-start(f32[1,1,512,128]{3,1,0,2:T(1,128)} %bitcast.38), calls=%async_computation.3 | async-start | bytes 524288 | tf_op jit(solution)/shard_map/all_to_all | solution.py:90
  31.2 10.9 %all-to-all-done.3 = f32[1,1,512,128]{3,1,0,2:T(1,128)S(1)} async-done(((f32[1,1,512,128]{3,1,0,2:T(1,128)}), f32[1,1,512,128]{3,1,0,2:T(1,128)S(1)}, u32[]{:S(2)}, u32[]{:S(2)}) %all-to-all-start.3) | async-done | bytes 262176 | tf_op jit(solution)/shard_map/all_to_all | solution.py:90
  42.1 3.6 all-to-all-start
  49.2 13.6 %all-to-all-done = f32[2,1,512,128]{3,0,1,2:T(2,128)S(1)} async-done(((f32[2,1,512,128]{3,0,1,2:T(2,128)}), f32[2,1,512,128]{3,0,1,2:T(2,128)S(1)}, u32[]{:S(2)}, u32[]{:S(2)}) %all-to-all-start) | async-done | bytes 524320 | tf_op jit(solution)/shard_map/all_to_all | solution.py:90
  62.7 3.7 all-to-all-start.4
  69.5 2.6 copy.222
  72.1 21.8 %all-to-all-done.4 = f32[1,2,32,32,128]{4,3,1,0,2:T(8,128)S(1)} async-done(((f32[1,2,32,32,128]{4,3,1,0,2:T(8,128)}), f32[1,2,32,32,128]{4,3,1,0,2:T(8,128)S(1)}, u32[]{:S(2)}, u32[]{:S(2)}) %all-to-all-start.4) | async-done | bytes 1048608 | tf_op jit(solution)/shard_map/all_to_all | solution.py:97
  93.9 4.2 all-to-all-start.1
  103.5 2.7 add_bitcast_fusion.3
  112.7 35.0 %all-to-all-done.1 = f32[2,2,32,32,128]{4,3,0,1,2:T(8,128)S(1)} async-done(((f32[2,2,32,32,128]{4,3,0,1,2:T(8,128)}), f32[2,2,32,32,128]{4,3,0,1,2:T(8,128)S(1)}, u32[]{:S(2)}, u32[]{:S(2)}) %all-to-all-start.1) | async-done | bytes 2097184 | tf_op jit(solution)/shard_map/all_to_all | solution.py:97
  148.1 2.7 fusion.27
  150.8 2.5 fusion.23
  153.3 2.6 fusion.5
  156.0 4.9 %multiply_subtract_fusion = (f32[2,2,4,128,128]{4,2,3,1,0:T(4,128)}, f32[2,2,4,128,128]{4,2,3,1,0:T(4,128)S(1)}) fusion(f32[2,2,4,128,128]{4,2,3,1,0:T(4,128)S(1)} %fusion.5, f32[4,128]{0,1:T(8,128)S(1)} %copy.230, f32[4,128]{0,1:T(8,128)S(1)} %copy-done.11, f32[2,2,128,128,4]{3,4,2,1,0:T(4,128)S(1)} %fusion.23, f32[2,2,4,128,128]{4,3,2,1,0:T(8,128)S(1)} %bitcast.367), kind=kOutput, calls=%fused_computation.63 | convolution fusion | flops 14418160 | bytes 5246976 | tf_op jit(solution)/shard_map/qa,fkabc->fkqbc/dot_general | solution.py:26
  161.2 2.2 fusion.70
  168.7 1.9 multiply_subtract_fusion.2
  180.0 2.1 fusion.6
  185.4 4.5 all-to-all-start.7
  197.8 2.1 fusion
  201.9 2.2 fusion.1
  204.3 13.0 %all-to-all-done.7 = f32[1,2,2,512,128]{4,2,1,0,3:T(2,128)} async-done(((f32[1,2,2,512,128]{4,2,1,0,3:T(2,128)}), f32[1,2,2,512,128]{4,2,1,0,3:T(2,128)}, u32[]{:S(2)}, u32[]{:S(2)}) %all-to-all-start.7) | async-done | bytes 1048608 | tf_op jit(solution)/shard_map/all_to_all | solution.py:113
  221.0 4.2 all-to-all-start.8
  225.7 3.0 copy.261
  228.7 4.9 %all-to-all-done.8 = bf16[1,16,32,128]{3,2,0,1:T(8,128)(2,1)} async-done(((bf16[1,16,32,128]{3,2,0,1:T(8,128)(2,1)}), bf16[1,16,32,128]{3,2,0,1:T(8,128)(2,1)}, u32[]{:S(2)}, u32[]{:S(2)}) %all-to-all-start.8) | async-done | bytes 131104 | tf_op jit(solution)/shard_map/all_to_all | solution.py:122
  233.6 3.7 all-to-all-start.5
  240.1 45.9 %all-to-all-done.5 = f32[2,2,2,512,128]{4,2,0,1,3:T(2,128)S(1)} async-done(((f32[2,2,2,512,128]{4,2,0,1,3:T(2,128)}), f32[2,2,2,512,128]{4,2,0,1,3:T(2,128)S(1)}, u32[]{:S(2)}, u32[]{:S(2)}) %all-to-all-start.5) | async-done | bytes 2097184 | tf_op jit(solution)/shard_map/all_to_all | solution.py:113
  286.0 3.9 all-to-all-start.9
  294.4 4.3 all-to-all-done.9
  298.7 3.7 all-to-all-start.6
  304.5 80.4 %all-reduce = bf16[2,64,64]{2,1,0:T(8,128)(2,1)S(1)} all-reduce(bf16[2,64,64]{2,1,0:T(8,128)(2,1)S(1)} %convolution_convert_fusion.2), channel_id=2, replica_groups=mesh['seq'=16,'ch'=16] {'seq'}, use_global_device_ids=true, to_apply=%region_0.1.clone | all-reduce | flops 8192 | bytes 32768
  385.9 74.6 %all-reduce.1 = f32[4,32,32]{2,0,1:T(4,128)S(1)} all-reduce(f32[4,32,32]{2,0,1:T(4,128)S(1)} %copy.283), channel_id=3, replica_groups=mesh['seq'=16,'ch'=16] {'seq'}, use_global_device_ids=true, to_apply=%region_1.2.clone | all-reduce | flops 4096 | bytes 32768
  (132 shorter events, 66.5 us)
Async XLA Ops:
  0.6 22.4 %copy-start = (bf16[2,64,64]{2,1,0:T(8,128)(2,1)S(1)}, bf16[2,64,64]{2,1,0:T(8,128)(2,1)}, u32[]{:S(2)}) copy-start(bf16[2,64,64]{2,1,0:T(8,128)(2,1)} %param.10) | copy-start | bytes 49156
  0.6 22.7 %copy-start.12 = (bf16[512,128]{1,0:T(8,128)(2,1)S(1)}, bf16[512,128]{1,0:T(8,128)(2,1)}, u32[]{:S(2)}) copy-start(bf16[512,128]{1,0:T(8,128)(2,1)} %param.8) | copy-start | bytes 393220
  0.7 29.2 %copy-start.14 = (bf16[512,128]{1,0:T(8,128)(2,1)S(1)}, bf16[512,128]{1,0:T(8,128)(2,1)}, u32[]{:S(2)}) copy-start(bf16[512,128]{1,0:T(8,128)(2,1)} %param.6) | copy-start | bytes 393220
  0.7 29.2 %copy-start.15 = (bf16[512,128]{1,0:T(8,128)(2,1)S(1)}, bf16[512,128]{1,0:T(8,128)(2,1)}, u32[]{:S(2)}) copy-start(bf16[512,128]{1,0:T(8,128)(2,1)} %param.7) | copy-start | bytes 393220
  1.7 22.3 %copy-start.6 = (bf16[512,128]{0,1:T(8,128)(2,1)}, bf16[512,128]{0,1:T(8,128)(2,1)S(1)}, u32[]{:S(2)}) copy-start(bf16[512,128]{0,1:T(8,128)(2,1)S(1)} %copy.233) | copy-start | bytes 393220
  23.0 1.1 copy-start.8
  24.1 18.1 %all-to-all-start.3 = ((f32[1,1,512,128]{3,1,0,2:T(1,128)}), f32[1,1,512,128]{3,1,0,2:T(1,128)S(1)}, u32[]{:S(2)}, u32[]{:S(2)}) async-start(f32[1,1,512,128]{3,1,0,2:T(1,128)} %bitcast.38), calls=%async_computation.3 | async-start | bytes 524288 | tf_op jit(solution)/shard_map/all_to_all | solution.py:90
  42.1 20.6 %all-to-all-start = ((f32[2,1,512,128]{3,0,1,2:T(2,128)}), f32[2,1,512,128]{3,0,1,2:T(2,128)S(1)}, u32[]{:S(2)}, u32[]{:S(2)}) async-start(f32[2,1,512,128]{3,0,1,2:T(2,128)} %maximum_bitcast_fusion), calls=%async_computation | async-start | bytes 1048576 | tf_op jit(solution)/shard_map/all_to_all | solution.py:90
  62.7 31.1 %all-to-all-start.4 = ((f32[1,2,32,32,128]{4,3,1,0,2:T(8,128)}), f32[1,2,32,32,128]{4,3,1,0,2:T(8,128)S(1)}, u32[]{:S(2)}, u32[]{:S(2)}) async-start(f32[1,2,32,32,128]{4,3,1,0,2:T(8,128)} %copy.240), calls=%async_computation.4 | async-start | bytes 2097152 | tf_op jit(solution)/shard_map/all_to_all | solution.py:97
  93.9 53.9 %all-to-all-start.1 = ((f32[2,2,32,32,128]{4,3,0,1,2:T(8,128)}), f32[2,2,32,32,128]{4,3,0,1,2:T(8,128)S(1)}, u32[]{:S(2)}, u32[]{:S(2)}) async-start(f32[2,2,32,32,128]{4,3,0,1,2:T(8,128)} %copy.222), calls=%async_computation.1 | async-start | bytes 4194304 | tf_op jit(solution)/shard_map/all_to_all | solution.py:97
  99.4 4.0 copy-start.10
  153.3 2.7 copy-start.11
  164.9 1.2 copy-start.2
  167.4 1.3 copy-start.4
  167.5 1.3 copy-start.5
  175.0 3.2 copy-start.3
  185.4 5.7 %copy-start.1 = (f32[1,2,4,128,128]{3,4,2,1,0:T(8,128)S(1)}, f32[1,2,4,128,128]{3,4,2,1,0:T(8,128)}, u32[]{:S(2)}) copy-start(f32[1,2,4,128,128]{3,4,2,1,0:T(8,128)} %get-tuple-element.37) | copy-start | bytes 1572868
  185.4 31.9 %all-to-all-start.7 = ((f32[1,2,2,512,128]{4,2,1,0,3:T(2,128)}), f32[1,2,2,512,128]{4,2,1,0,3:T(2,128)}, u32[]{:S(2)}, u32[]{:S(2)}) async-start(f32[1,2,2,512,128]{4,2,1,0,3:T(2,128)} %copy.273), calls=%async_computation.7 | async-start | bytes 2097152 | tf_op jit(solution)/shard_map/all_to_all | solution.py:113
  221.0 12.6 %all-to-all-start.8 = ((bf16[1,16,32,128]{3,2,0,1:T(8,128)(2,1)}), bf16[1,16,32,128]{3,2,0,1:T(8,128)(2,1)}, u32[]{:S(2)}, u32[]{:S(2)}) async-start(bf16[1,16,32,128]{3,2,0,1:T(8,128)(2,1)} %copy.276), calls=%async_computation.8 | async-start | bytes 262144 | tf_op jit(solution)/shard_map/all_to_all | solution.py:122
  228.7 8.6 %copy-start.13 = (bf16[512,128]{1,0:T(8,128)(2,1)S(1)}, bf16[512,128]{1,0:T(8,128)(2,1)}, u32[]{:S(2)}) copy-start(bf16[512,128]{1,0:T(8,128)(2,1)} %param.8) | copy-start | bytes 393220
  233.6 52.4 %all-to-all-start.5 = ((f32[2,2,2,512,128]{4,2,0,1,3:T(2,128)}), f32[2,2,2,512,128]{4,2,0,1,3:T(2,128)S(1)}, u32[]{:S(2)}, u32[]{:S(2)}) async-start(f32[2,2,2,512,128]{4,2,0,1,3:T(2,128)} %copy.261), calls=%async_computation.5 | async-start | bytes 4194304 | tf_op jit(solution)/shard_map/all_to_all | solution.py:113
  286.0 12.7 %all-to-all-start.9 = ((bf16[512,2,64]{0,1,2:T(2,128)(2,1)}), bf16[512,2,64]{0,1,2:T(2,128)(2,1)S(1)}, u32[]{:S(2)}, u32[]{:S(2)}) async-start(bf16[512,2,64]{0,1,2:T(2,128)(2,1)} %copy.281), calls=%async_computation.9 | async-start | bytes 262144 | tf_op jit(solution)/shard_map/all_to_all | solution.py:151
  292.7 9.7 %copy-start.16 = (u32[256]{0:T(256)S(1)}, u32[256]{0:T(256)}, u32[]{:S(2)}) copy-start(u32[256]{0:T(256)} %constant.160) | copy-start | bytes 3076
  292.7 11.6 %copy-start.9 = (bf16[512,64,2]{0,1,2:T(8,128)(2,1)S(1)}, bf16[512,64,2]{0,1,2:T(8,128)(2,1)}, u32[]{:S(2)}) copy-start(bf16[512,64,2]{0,1,2:T(8,128)(2,1)} %copy-done.8) | copy-start | bytes 393220
  292.7 93.0 %copy-start.7 = (bf16[512,128]{0,1:T(8,128)(2,1)S(1)}, bf16[512,128]{0,1:T(8,128)(2,1)}, u32[]{:S(2)}) copy-start(bf16[512,128]{0,1:T(8,128)(2,1)} %copy-done.6) | copy-start | bytes 393220
  298.7 162.4 %all-to-all-start.6 = ((f32[2,16,32,128]{3,2,0,1:T(8,128)}), f32[2,16,32,128]{3,2,0,1:T(8,128)S(1)}, u32[]{:S(2)}, u32[]{:S(2)}) async-start(f32[2,16,32,128]{3,2,0,1:T(8,128)} %copy.264), calls=%async_computation.6 | async-start | bytes 1048576 | tf_op jit(solution)/shard_map/all_to_all | solution.py:122
where the time goes:
time: 470 us; the launch traced here: 463 us
  blocking collectives  175 us (37%)
  waiting for transfers between devices  149 us (32%)
  matrix products  63.8 us (14%)
  starting transfers between devices  37.1 us (8%)
  local copies, waits for them, and re-layouts  27.6 us (6%)
  other arithmetic  6.55 us (1%)
    unnamed x2, blocking collectives  155 us
    all_to_all x2, waiting for transfers between devices, inverse_transform(): lax.all_to_all(jnp.stack([real_part, imag_part], axis=1), 'seq', split_ax...  58.9 us
    all_to_all x2, waiting for transfers between devices, forward_transform(): lax.all_to_all(jnp.stack([real_part, imag_part], axis=1), 'seq', split_ax...  56.8 us
    all_to_all x2, waiting for transfers between devices, forward_transform(): lax.all_to_all(fields[:, None], 'seq', split_axis=2, concat_axis=1, tiled...  24.5 us
    all_to_all x1, blocking collectives, shards(): lax.all_to_all(second_back, 'ch', split_axis=2, concat_axis=1, tiled=True)  20.1 us
    dot_general x8, matrix products, contract(): jnp.einsum(form, sine, real_part, precision=HIGHEST)  15.6 us
    dot_general x8, matrix products, contract(): jnp.einsum(form, sine, imag_part, precision=HIGHEST)  14.7 us
    dot_general x8, matrix products, contract(): jnp.einsum(form, cosine, imag_part, precision=HIGHEST)  13.5 us
  transfers between devices with their start and end apart: 9, of which 8 were waited for; matrix products, arithmetic and copies ran while one was open for 11% of the time, Pallas kernels for 0%

commit v1 on v0

--- a/solution.py
+++ b/solution.py
@@ -154,7 +154,10 @@
         "tko,kio->tki", incoming, w_second, preferred_element_type=jnp.float32
     ).astype(jnp.bfloat16)
     grad_second = jnp.einsum("tik,tko->kio", received, incoming, preferred_element_type=jnp.float32)
-    returned = lax.all_to_all(second_back, "ch", split_axis=2, concat_axis=1, tiled=True)
+    returned = jnp.concatenate(
+        lax.all_to_all(jnp.stack(jnp.split(second_back, lax.axis_size("ch"), axis=2)), "ch", 0, 0),
+        axis=1,
+    )
     grad_product = jnp.einsum(
         "tki,ijk->tij", returned, w_first, preferred_element_type=jnp.float32
     ).reshape(rows, width)

time: 470 us -> 471 us (level)
  no operation moved by 1% of the time
where the time goes in v1:
time: 471 us; the launch traced here: 463 us
  blocking collectives  175 us (37%)
  waiting for transfers between devices  149 us (32%)
  matrix products  63.8 us (14%)
  starting transfers between devices  37.2 us (8%)
  local copies, waits for them, and re-layouts  28.2 us (6%)
  other arithmetic  6.55 us (1%)
    unnamed x2, blocking collectives  155 us
    all_to_all x2, waiting for transfers between devices, inverse_transform(): lax.all_to_all(jnp.stack([real_part, imag_part], axis=1), 'seq', split_ax...  58.9 us
    all_to_all x2, waiting for transfers between devices, forward_transform(): lax.all_to_all(jnp.stack([real_part, imag_part], axis=1), 'seq', split_ax...  56.8 us
    all_to_all x2, waiting for transfers between devices, forward_transform(): lax.all_to_all(fields[:, None], 'seq', split_axis=2, concat_axis=1, tiled...  24.5 us
    all_to_all x1, blocking collectives, shards(): lax.all_to_all(jnp.stack(jnp.split(second_back, lax.axis_size('ch'), axis...  20.1 us
    dot_general x8, matrix products, contract(): jnp.einsum(form, sine, real_part, precision=HIGHEST)  15.6 us
    dot_general x8, matrix products, contract(): jnp.einsum(form, sine, imag_part, precision=HIGHEST)  14.7 us
    dot_general x8, matrix products, contract(): jnp.einsum(form, cosine, imag_part, precision=HIGHEST)  13.5 us
  transfers between devices with their start and end apart: 9, of which 8 were waited for; matrix products, arithmetic and copies ran while one was open for 11% of the time, Pallas kernels for 0%

profile of v1, /device:TPU:8, one launch (start us, length us, event | category | flops | bytes accessed | tf_op | source)
XLA Modules:
  0.0 463.3 jit_solution(17433466280358369679)
XLA Ops:
  3.0 20.1 %all_to_all.134 = bf16[16,512,4,2]{1,3,2,0:T(2,128)(2,1)S(1)} all-to-all(bf16[16,512,4,2]{1,3,2,0:T(2,128)(2,1)S(1)} %constant_dynamic-update-slice_fusion), channel_id=1, replica_groups=mesh['seq'=16,'ch'=16] {'ch'}, dimensions={0} | all-to-all | bytes 262144 | tf_op jit(solution)/shard_map/all_to_all | solution.py:158
  24.7 5.8 %all-to-all-start.3 = ((f32[1,1,512,128]{3,1,0,2:T(1,128)}), f32[1,1,512,128]{3,1,0,2:T(1,128)S(1)}, u32[]{:S(2)}, u32[]{:S(2)}) async-start(f32[1,1,512,128]{3,1,0,2:T(1,128)} %bitcast.54), calls=%async_computation.3 | async-start | bytes 524288 | tf_op jit(solution)/shard_map/all_to_all | solution.py:90
  31.8 10.9 %all-to-all-done.3 = f32[1,1,512,128]{3,1,0,2:T(1,128)S(1)} async-done(((f32[1,1,512,128]{3,1,0,2:T(1,128)}), f32[1,1,512,128]{3,1,0,2:T(1,128)S(1)}, u32[]{:S(2)}, u32[]{:S(2)}) %all-to-all-start.3) | async-done | bytes 262176 | tf_op jit(solution)/shard_map/all_to_all | solution.py:90
  42.7 3.6 all-to-all-start
  49.8 13.6 %all-to-all-done = f32[2,1,512,128]{3,0,1,2:T(2,128)S(1)} async-done(((f32[2,1,512,128]{3,0,1,2:T(2,128)}), f32[2,1,512,128]{3,0,1,2:T(2,128)S(1)}, u32[]{:S(2)}, u32[]{:S(2)}) %all-to-all-start) | async-done | bytes 524320 | tf_op jit(solution)/shard_map/all_to_all | solution.py:90
  63.3 3.7 all-to-all-start.4
  70.1 2.6 copy.224
  72.7 21.8 %all-to-all-done.4 = f32[1,2,32,32,128]{4,3,1,0,2:T(8,128)S(1)} async-done(((f32[1,2,32,32,128]{4,3,1,0,2:T(8,128)}), f32[1,2,32,32,128]{4,3,1,0,2:T(8,128)S(1)}, u32[]{:S(2)}, u32[]{:S(2)}) %all-to-all-start.4) | async-done | bytes 1048608 | tf_op jit(solution)/shard_map/all_to_all | solution.py:97
  94.5 4.2 all-to-all-start.1
  104.1 2.7 add_bitcast_fusion.3
  113.4 35.0 %all-to-all-done.1 = f32[2,2,32,32,128]{4,3,0,1,2:T(8,128)S(1)} async-done(((f32[2,2,32,32,128]{4,3,0,1,2:T(8,128)}), f32[2,2,32,32,128]{4,3,0,1,2:T(8,128)S(1)}, u32[]{:S(2)}, u32[]{:S(2)}) %all-to-all-start.1) | async-done | bytes 2097184 | tf_op jit(solution)/shard_map/all_to_all | solution.py:97
  148.7 2.7 fusion.27
  151.4 2.5 fusion.23
  153.9 2.6 fusion.5
  156.6 4.9 %multiply_subtract_fusion = (f32[2,2,4,128,128]{4,2,3,1,0:T(4,128)}, f32[2,2,4,128,128]{4,2,3,1,0:T(4,128)S(1)}) fusion(f32[2,2,4,128,128]{4,2,3,1,0:T(4,128)S(1)} %fusion.5, f32[4,128]{0,1:T(8,128)S(1)} %copy.232, f32[4,128]{0,1:T(8,128)S(1)} %copy-done.9, f32[2,2,128,128,4]{3,4,2,1,0:T(4,128)S(1)} %fusion.23, f32[2,2,4,128,128]{4,3,2,1,0:T(8,128)S(1)} %bitcast.426), kind=kOutput, calls=%fused_computation.63 | convolution fusion | flops 14418160 | bytes 5246976 | tf_op jit(solution)/shard_map/qa,fkabc->fkqbc/dot_general | solution.py:26
  161.8 2.2 fusion.73
  169.3 1.9 multiply_subtract_fusion.2
  180.6 2.1 fusion.6
  186.1 4.5 all-to-all-start.7
  198.4 2.1 fusion
  202.5 2.2 fusion.1
  204.9 13.0 %all-to-all-done.7 = f32[1,2,2,512,128]{4,2,1,0,3:T(2,128)} async-done(((f32[1,2,2,512,128]{4,2,1,0,3:T(2,128)}), f32[1,2,2,512,128]{4,2,1,0,3:T(2,128)}, u32[]{:S(2)}, u32[]{:S(2)}) %all-to-all-start.7) | async-done | bytes 1048608 | tf_op jit(solution)/shard_map/all_to_all | solution.py:113
  221.6 4.2 all-to-all-start.8
  226.3 3.0 copy.262
  229.3 4.9 %all-to-all-done.8 = bf16[1,16,32,128]{3,2,0,1:T(8,128)(2,1)} async-done(((bf16[1,16,32,128]{3,2,0,1:T(8,128)(2,1)}), bf16[1,16,32,128]{3,2,0,1:T(8,128)(2,1)}, u32[]{:S(2)}, u32[]{:S(2)}) %all-to-all-start.8) | async-done | bytes 131104 | tf_op jit(solution)/shard_map/all_to_all | solution.py:122
  234.2 3.7 all-to-all-start.5
  240.7 45.9 %all-to-all-done.5 = f32[2,2,2,512,128]{4,2,0,1,3:T(2,128)S(1)} async-done(((f32[2,2,2,512,128]{4,2,0,1,3:T(2,128)}), f32[2,2,2,512,128]{4,2,0,1,3:T(2,128)S(1)}, u32[]{:S(2)}, u32[]{:S(2)}) %all-to-all-start.5) | async-done | bytes 2097184 | tf_op jit(solution)/shard_map/all_to_all | solution.py:113
  286.6 3.9 all-to-all-start.9
  295.0 4.3 all-to-all-done.9
  299.3 3.7 all-to-all-start.6
  305.1 80.4 %all-reduce = bf16[2,64,64]{2,1,0:T(8,128)(2,1)S(1)} all-reduce(bf16[2,64,64]{2,1,0:T(8,128)(2,1)S(1)} %convolution_convert_fusion.2), channel_id=2, replica_groups=mesh['seq'=16,'ch'=16] {'seq'}, use_global_device_ids=true, to_apply=%region_0.1.clone | all-reduce | flops 8192 | bytes 32768
  386.5 74.6 %all-reduce.1 = f32[4,32,32]{2,0,1:T(4,128)S(1)} all-reduce(f32[4,32,32]{2,0,1:T(4,128)S(1)} %copy.285), channel_id=3, replica_groups=mesh['seq'=16,'ch'=16] {'seq'}, use_global_device_ids=true, to_apply=%region_1.2.clone | all-reduce | flops 4096 | bytes 32768
  (145 shorter events, 67.0 us)
Async XLA Ops:
  0.6 22.5 %copy-start = (bf16[2,64,64]{2,1,0:T(8,128)(2,1)S(1)}, bf16[2,64,64]{2,1,0:T(8,128)(2,1)}, u32[]{:S(2)}) copy-start(bf16[2,64,64]{2,1,0:T(8,128)(2,1)} %param.10) | copy-start | bytes 49156
  0.6 23.3 %copy-start.10 = (bf16[512,128]{1,0:T(8,128)(2,1)S(1)}, bf16[512,128]{1,0:T(8,128)(2,1)}, u32[]{:S(2)}) copy-start(bf16[512,128]{1,0:T(8,128)(2,1)} %param.8) | copy-start | bytes 393220
  0.7 29.8 %copy-start.14 = (bf16[512,128]{1,0:T(8,128)(2,1)S(1)}, bf16[512,128]{1,0:T(8,128)(2,1)}, u32[]{:S(2)}) copy-start(bf16[512,128]{1,0:T(8,128)(2,1)} %param.6) | copy-start | bytes 393220
  0.7 29.8 %copy-start.15 = (bf16[512,128]{1,0:T(8,128)(2,1)S(1)}, bf16[512,128]{1,0:T(8,128)(2,1)}, u32[]{:S(2)}) copy-start(bf16[512,128]{1,0:T(8,128)(2,1)} %param.7) | copy-start | bytes 393220
  1.7 22.9 %copy-start.6 = (bf16[512,128]{0,1:T(8,128)(2,1)}, bf16[512,128]{0,1:T(8,128)(2,1)S(1)}, u32[]{:S(2)}) copy-start(bf16[512,128]{0,1:T(8,128)(2,1)S(1)} %copy.235) | copy-start | bytes 393220
  23.1 0.7 copy-start.12
  24.7 18.1 %all-to-all-start.3 = ((f32[1,1,512,128]{3,1,0,2:T(1,128)}), f32[1,1,512,128]{3,1,0,2:T(1,128)S(1)}, u32[]{:S(2)}, u32[]{:S(2)}) async-start(f32[1,1,512,128]{3,1,0,2:T(1,128)} %bitcast.54), calls=%async_computation.3 | async-start | bytes 524288 | tf_op jit(solution)/shard_map/all_to_all | solution.py:90
  42.7 20.6 %all-to-all-start = ((f32[2,1,512,128]{3,0,1,2:T(2,128)}), f32[2,1,512,128]{3,0,1,2:T(2,128)S(1)}, u32[]{:S(2)}, u32[]{:S(2)}) async-start(f32[2,1,512,128]{3,0,1,2:T(2,128)} %maximum_bitcast_fusion), calls=%async_computation | async-start | bytes 1048576 | tf_op jit(solution)/shard_map/all_to_all | solution.py:90
  63.3 31.1 %all-to-all-start.4 = ((f32[1,2,32,32,128]{4,3,1,0,2:T(8,128)}), f32[1,2,32,32,128]{4,3,1,0,2:T(8,128)S(1)}, u32[]{:S(2)}, u32[]{:S(2)}) async-start(f32[1,2,32,32,128]{4,3,1,0,2:T(8,128)} %copy.241), calls=%async_computation.4 | async-start | bytes 2097152 | tf_op jit(solution)/shard_map/all_to_all | solution.py:97
  94.5 53.9 %all-to-all-start.1 = ((f32[2,2,32,32,128]{4,3,0,1,2:T(8,128)}), f32[2,2,32,32,128]{4,3,0,1,2:T(8,128)S(1)}, u32[]{:S(2)}, u32[]{:S(2)}) async-start(f32[2,2,32,32,128]{4,3,0,1,2:T(8,128)} %copy.224), calls=%async_computation.1 | async-start | bytes 4194304 | tf_op jit(solution)/shard_map/all_to_all | solution.py:97
  100.1 4.0 copy-start.8
  153.9 2.7 copy-start.9
  165.6 1.2 copy-start.2
  168.1 1.3 copy-start.4
  168.1 1.3 copy-start.5
  175.6 3.2 copy-start.3
  186.1 5.7 %copy-start.1 = (f32[1,2,4,128,128]{3,4,2,1,0:T(8,128)S(1)}, f32[1,2,4,128,128]{3,4,2,1,0:T(8,128)}, u32[]{:S(2)}) copy-start(f32[1,2,4,128,128]{3,4,2,1,0:T(8,128)} %get-tuple-element.37) | copy-start | bytes 1572868
  186.1 31.9 %all-to-all-start.7 = ((f32[1,2,2,512,128]{4,2,1,0,3:T(2,128)}), f32[1,2,2,512,128]{4,2,1,0,3:T(2,128)}, u32[]{:S(2)}, u32[]{:S(2)}) async-start(f32[1,2,2,512,128]{4,2,1,0,3:T(2,128)} %copy.274), calls=%async_computation.7 | async-start | bytes 2097152 | tf_op jit(solution)/shard_map/all_to_all | solution.py:113
  221.6 12.6 %all-to-all-start.8 = ((bf16[1,16,32,128]{3,2,0,1:T(8,128)(2,1)}), bf16[1,16,32,128]{3,2,0,1:T(8,128)(2,1)}, u32[]{:S(2)}, u32[]{:S(2)}) async-start(bf16[1,16,32,128]{3,2,0,1:T(8,128)(2,1)} %copy.277), calls=%async_computation.8 | async-start | bytes 262144 | tf_op jit(solution)/shard_map/all_to_all | solution.py:122
  229.3 8.6 %copy-start.11 = (bf16[512,128]{1,0:T(8,128)(2,1)S(1)}, bf16[512,128]{1,0:T(8,128)(2,1)}, u32[]{:S(2)}) copy-start(bf16[512,128]{1,0:T(8,128)(2,1)} %param.8) | copy-start | bytes 393220
  234.2 52.4 %all-to-all-start.5 = ((f32[2,2,2,512,128]{4,2,0,1,3:T(2,128)}), f32[2,2,2,512,128]{4,2,0,1,3:T(2,128)S(1)}, u32[]{:S(2)}, u32[]{:S(2)}) async-start(f32[2,2,2,512,128]{4,2,0,1,3:T(2,128)} %copy.262), calls=%async_computation.5 | async-start | bytes 4194304 | tf_op jit(solution)/shard_map/all_to_all | solution.py:113
  286.6 12.7 %all-to-all-start.9 = ((bf16[512,2,64]{0,1,2:T(2,128)(2,1)}), bf16[512,2,64]{0,1,2:T(2,128)(2,1)S(1)}, u32[]{:S(2)}, u32[]{:S(2)}) async-start(bf16[512,2,64]{0,1,2:T(2,128)(2,1)} %copy.283), calls=%async_computation.9 | async-start | bytes 262144 | tf_op jit(solution)/shard_map/all_to_all | solution.py:151
  293.3 9.7 %copy-start.16 = (u32[256]{0:T(256)S(1)}, u32[256]{0:T(256)}, u32[]{:S(2)}) copy-start(u32[256]{0:T(256)} %constant.160) | copy-start | bytes 3076
  293.3 11.6 %copy-start.13 = (bf16[16,512,4,2]{1,3,2,0:T(2,128)(2,1)S(1)}, bf16[16,512,4,2]{1,3,2,0:T(2,128)(2,1)}, u32[]{:S(2)}) copy-start(bf16[16,512,4,2]{1,3,2,0:T(2,128)(2,1)} %copy-done.12) | copy-start | bytes 393220
  293.3 93.0 %copy-start.7 = (bf16[512,128]{0,1:T(8,128)(2,1)S(1)}, bf16[512,128]{0,1:T(8,128)(2,1)}, u32[]{:S(2)}) copy-start(bf16[512,128]{0,1:T(8,128)(2,1)} %copy-done.6) | copy-start | bytes 393220
  299.3 162.4 %all-to-all-start.6 = ((f32[2,16,32,128]{3,2,0,1:T(8,128)}), f32[2,16,32,128]{3,2,0,1:T(8,128)S(1)}, u32[]{:S(2)}, u32[]{:S(2)}) async-start(f32[2,16,32,128]{3,2,0,1:T(8,128)} %copy.265), calls=%async_computation.6 | async-start | bytes 1048576 | tf_op jit(solution)/shard_map/all_to_all | solution.py:122
